TPU v7x, 32 devices: a whole 2x2x4 slice. The times are simulated.
32 devices in a mesh: row: 8 (over y, x, core), col: 4 (over z).
Axes of the slice: x: 2, y: 2, z: 4, core: 2. Of those that a mesh axis runs over, the one named last changes fastest.
Arguments:
- amplitudes: bfloat16 [24576, 24576], P('col', 'row'), may hold values from -0.0390625 to 0.0390625
- cholesky: bfloat16 [24576, 1280], P(('row', 'col')), may hold values from -5 to 5
- occ_map: int32 [24576], replicated, may hold values from 0 to 47
- vir_map: int32 [24576], replicated, may hold values from 0 to 511
Outputs:
- new_amplitudes: bfloat16 [24576, 24576], P('col', 'row')
All inputs are finite; a program needn't handle non-finite values.
Results may differ from a plain program's by a relative error of at most 0.0056.
Values may be sent and summed in bfloat16 or wider, within the bound.
No kernel may reach another device: no remote copies, remote signals or barrier semaphores. Data moves between devices by JAX's collectives and lax.ppermute only.
A program may use at most 192 MiB of HBM per device.

v0:
```python
import jax
import jax.numpy as jnp
from jax import lax
from jax.sharding import PartitionSpec as P

NOCC = 48
NVIR = 512


def broadcast(x, axis, root):
    mine = lax.axis_index(axis) == root
    return lax.psum(jnp.where(mine, x, jnp.zeros_like(x)), axis)


def pair_gap(occ_map, vir_map):
    occ = occ_map.astype(jnp.float32)
    vir = vir_map.astype(jnp.float32)
    return 0.5 + 2.5 * jnp.sqrt(vir / NVIR) + (0.5 + 2.5 * occ / NOCC)


def body(amplitudes, cholesky, occ_map, vir_map):
    tile_rows, tile_cols = amplitudes.shape
    row_index = lax.axis_index("row")
    col_index = lax.axis_index("col")
    q_start = row_index * tile_cols
    p_start = col_index * tile_rows
    offset = q_start - p_start
    on_diag = jnp.logical_and(offset >= 0, offset < tile_rows).astype(jnp.float32)
    safe_offset = jnp.clip(offset, 0, tile_rows - tile_cols)
    piece = lax.all_gather(cholesky, "col", axis=0, tiled=True)
    count = piece.shape[0]
    total = jnp.dot(amplitudes, piece, preferred_element_type=jnp.float32)
    current = lax.dynamic_slice_in_dim(total, safe_offset, count, 0)
    partial_value = lax.dynamic_update_slice_in_dim(
        total, current + on_diag * piece.astype(jnp.float32), safe_offset, 0
    )
    y_share = lax.psum_scatter(partial_value, "row", scatter_dimension=0, tiled=True).astype(
        jnp.bfloat16
    )
    y_block = lax.all_gather(y_share, "row", axis=0, tiled=True)
    q_root = q_start // tile_rows
    q_inside = q_start % tile_rows
    own_part = lax.dynamic_slice_in_dim(y_block, q_inside, tile_cols, 0)
    y_cols = broadcast(own_part, "col", q_root)
    cycle = lax.dot_general(
        y_block, y_cols, (((1,), (1,)), ((), ())), preferred_element_type=jnp.float32
    )
    gap_rows = pair_gap(
        lax.dynamic_slice_in_dim(occ_map, p_start, tile_rows, 0),
        lax.dynamic_slice_in_dim(vir_map, p_start, tile_rows, 0),
    )
    gap_cols = pair_gap(
        lax.dynamic_slice_in_dim(occ_map, q_start, tile_cols, 0),
        lax.dynamic_slice_in_dim(vir_map, q_start, tile_cols, 0),
    )
    return (-cycle / (gap_rows[:, None] + gap_cols[None, :])).astype(jnp.bfloat16)


def solution(mesh):
    return jax.shard_map(
        body,
        mesh=mesh,
        in_specs=(P("col", "row"), P(("row", "col"), None), P(), P()),
        out_specs=P("col", "row"),
        check_vma=False,
    )
```

profile of v0, /device:TPU:0, one launch (start us, length us, event | category | flops | bytes accessed | tf_op | source)
XLA Modules:
  0.0 884.4 jit_solution(14098019015922236109)
XLA Ops:
  6.5 0.0 all-gather.3.cloned.1.call-start
  6.5 0.7 all-gather.3.cloned.1.call-update
  7.3 0.0 reduce-scatter.2.cloned.1.call-start
  7.3 145.4 %all-gather.3.cloned.1.call-done = bf16[3072,1280]{1,0:T(8,128)(2,1)} async-done(((bf16[768,1280]{1,0:T(8,128)(2,1)}), bf16[3072,1280]{1,0:T(8,128)(2,1)}) %all-gather.3.cloned.1.call-update) | async-done | bytes 7864336 | tf_op jit(solution)/shard_map/all_gather | solution.py:30
  152.7 0.0 copy-start
  152.7 58.6 %fusion = f32[6144,1280]{1,0:T(8,128)} fusion(bf16[6144,3072]{1,0:T(8,128)(2,1)} %param.4, bf16[3072,1280]{1,0:T(8,128)(2,1)} %all-gather.3.cloned.1.call-done), kind=kOutput, calls=%fused_computation.5 | convolution fusion | flops 48318382080 | bytes 77070336 | tf_op jit(solution)/shard_map/dot_general | solution.py:32
  211.3 0.0 copy-done
  211.3 11.6 %multiply_add_fusion = f32[3072,1280]{1,0:T(8,128)} fusion(bf16[3072,1280]{1,0:T(8,128)(2,1)S(1)} %copy-done, f32[6144,1280]{1,0:T(8,128)} %fusion, s32[]{:T(128)S(6)} %min.4, f32[]{:T(128)S(6)} %convert_element_type.24), kind=kLoop, calls=%fused_computation.1 | loop fusion | flops 11796480 | bytes 39321608 | tf_op jit(solution)/shard_map/add | solution.py:35
  222.9 36.3 %dynamic_update_slice.3 = f32[6144,1280]{1,0:T(8,128)} dynamic-update-slice(f32[6144,1280]{1,0:T(8,128)} %fusion, f32[3072,1280]{1,0:T(8,128)} %multiply_add_fusion, s32[]{:T(128)S(6)} %min.4, s32[]{:T(128)} %constant.40.clone.1) | dynamic-update-slice | bytes 31457284 | tf_op jit(solution)/shard_map/dynamic_update_slice | solution.py:34
  259.2 0.0 reduce-scatter.2.cloned.1.call-update
  259.2 0.0 all-gather.5.cloned.1.call-start
  259.3 190.0 %reduce-scatter.2.cloned.1.call-done = f32[768,1280]{1,0:T(8,128)} async-done(((f32[6144,1280]{1,0:T(8,128)}), f32[768,1280]{1,0:T(8,128)}) %reduce-scatter.2.cloned.1.call-update) | async-done | bytes 3932176 | tf_op jit(solution)/shard_map/reduce_scatter | solution.py:37
  449.3 3.6 convert_element_type.26
  452.8 0.0 all-gather.5.cloned.1.call-update
  452.9 0.2 all-reduce.2.cloned.1.call-start
  453.1 85.2 %all-gather.5.cloned.1.call-done = bf16[6144,1280]{1,0:T(8,128)(2,1)} async-done(((bf16[768,1280]{1,0:T(8,128)(2,1)}), bf16[6144,1280]{1,0:T(8,128)(2,1)}) %all-gather.5.cloned.1.call-update) | async-done | bytes 15728656 | tf_op jit(solution)/shard_map/all_gather | solution.py:40
  538.3 8.8 dynamic-slice_select_fusion
  547.2 0.0 all-reduce.2.cloned.1.call-update
  547.2 0.7 add_add_fusion.1
  547.9 0.8 add_add_fusion
  548.7 272.4 %all-reduce.2.cloned.1.call-done = bf16[3072,1280]{1,0:T(8,128)(2,1)} async-done(((bf16[3072,1280]{1,0:T(8,128)(2,1)}), bf16[3072,1280]{1,0:T(8,128)(2,1)}) %all-reduce.2.cloned.1.call-update) | async-done | bytes 7864336 | tf_op jit(solution)/shard_map/psum | solution.py:12
  821.1 56.7 %divide_convert_fusion = bf16[6144,3072]{1,0:T(8,128)(2,1)} fusion(bf16[6144,1280]{1,0:T(8,128)(2,1)} %all-gather.5.cloned.1.call-done, bf16[3072,1280]{1,0:T(8,128)(2,1)} %all-reduce.2.cloned.1.call-done, f32[3072]{0:T(1024)S(1)} %add_add_fusion.1, f32[6144]{0:T(1024)S(1)} %add_add_fusion), kind=kOutput, calls=%fused_computation | convolution fusion | flops 48393879552 | bytes 61378560 | tf_op jit(solution)/shard_map/dot_general | solution.py:45
Async XLA Ops:
  6.5 146.2 %all-gather.3.cloned.1.call-start = ((), (), s32[]{:S(2)}) async-start(), calls=%async_computation.1 | async-start | bytes 9830400 | tf_op jit(solution)/shard_map/all_gather | solution.py:30
  7.3 442.0 %reduce-scatter.2.cloned.1.call-start = ((), (), s32[]{:S(2)}) async-start(), calls=%async_computation.2 | async-start | bytes 35389440 | tf_op jit(solution)/shard_map/reduce_scatter | solution.py:37
  152.7 58.6 %copy-start = (bf16[3072,1280]{1,0:T(8,128)(2,1)S(1)}, bf16[3072,1280]{1,0:T(8,128)(2,1)}, u32[]{:S(2)}) copy-start(bf16[3072,1280]{1,0:T(8,128)(2,1)} %all-gather.3.cloned.1.call-done) | copy-start | bytes 23592964
  259.2 279.1 %all-gather.5.cloned.1.call-start = ((), (), s32[]{:S(2)}) async-start(), calls=%async_computation.3 | async-start | bytes 17694720 | tf_op jit(solution)/shard_map/all_gather | solution.py:40
  452.9 368.2 %all-reduce.2.cloned.1.call-start = ((), (), s32[]{:S(2)}) async-start(), calls=%async_computation.4 | async-start | bytes 15728640 | tf_op jit(solution)/shard_map/psum | solution.py:12
Sparse Core Ops, SparseCore 0:
  8.9 143.7 all-gather.2
  259.4 189.8 reduce-scatter.1
  453.0 85.3 all-gather.4
  547.3 273.7 all-reduce.1
where the time goes:
time: 886 us; the launch traced here: 884 us
  waiting for transfers between devices  694 us (78%)
  matrix products  115 us (13%)
  local copies, waits for them, and re-layouts  36.3 us (4%)
  other arithmetic  25.5 us (3%)
  between operations  13.2 us (1%)
    psum x1, waiting for transfers between devices, broadcast(): return lax.psum(jnp.where(mine, x, jnp.zeros_like(x)), axis)  272 us
    reduce_scatter x1, waiting for transfers between devices, body(): lax.psum_scatter(partial_value, 'row', scatter_dimension=0, tiled=True)  190 us
    all_gather x1, waiting for transfers between devices, body(): piece = lax.all_gather(cholesky, 'col', axis=0, tiled=True)  145 us
    all_gather x1, waiting for transfers between devices, body(): y_block = lax.all_gather(y_share, 'row', axis=0, tiled=True)  85.2 us
    dot_general x1, matrix products, body(): total = jnp.dot(amplitudes, piece, preferred_element_type=jnp.float32)  58.6 us
    dot_general x1, matrix products, body(): lax.dot_general(y_block, y_cols, (((1,), (1,)), ((), ())), preferred_elem...  56.7 us
    dynamic_update_slice x1, local copies, waits for them, and re-layouts, body(): lax.dynamic_update_slice_in_dim(total, current + on_diag * piece.astype(j...  36.3 us
  transfers between devices with their start and end apart: 4, of which 4 were waited for; matrix products, arithmetic and copies ran while one was open for 0% of the time, Pallas kernels for 0%

commit v1 on v0

--- a/solution.py
+++ b/solution.py
@@ -5,6 +5,12 @@
 
 NOCC = 48
 NVIR = 512
+
+
+def laid_out(blocks, dim):
+    blocks = jnp.moveaxis(blocks, 0, dim)
+    dims = blocks.shape
+    return blocks.reshape(*dims[:dim], dims[dim] * dims[dim + 1], *dims[dim + 2 :])
 
 
 def broadcast(x, axis, root):
@@ -27,7 +33,19 @@
     offset = q_start - p_start
     on_diag = jnp.logical_and(offset >= 0, offset < tile_rows).astype(jnp.float32)
     safe_offset = jnp.clip(offset, 0, tile_rows - tile_cols)
-    piece = lax.all_gather(cholesky, "col", axis=0, tiled=True)
+    count_2 = lax.axis_size("col")
+    pairs = [(i, (i + 1) % count_2) for i in range(count_2)]
+    back = [(b, a) for a, b in pairs]
+    lower, upper = ([], [])
+    for step in range(count_2 - 1):
+        if step % 2 == 0:
+            lower.append(lax.ppermute(lower[-1] if lower else cholesky, "col", pairs))
+        else:
+            upper.append(lax.ppermute(upper[-1] if upper else cholesky, "col", back))
+    pieces = jnp.stack([*lower[::-1], cholesky, *upper])
+    shift = lax.axis_index("col") - len(lower)
+    pieces = pieces[(jnp.arange(count_2) - shift) % count_2]
+    piece = laid_out(pieces, 0)
     count = piece.shape[0]
     total = jnp.dot(amplitudes, piece, preferred_element_type=jnp.float32)
     current = lax.dynamic_slice_in_dim(total, safe_offset, count, 0)

time: 886 us -> 934 us (1.054)
  local copies, waits for them, and re-layouts: 36.3 us -> 86.5 us
  waiting for transfers between devices: 694 us -> 670 us
  other arithmetic: 25.5 us -> 35.7 us
    all_gather x1 -> x0, waiting for transfers between devices: 145 us -> none  [body(): piece = lax.all_gather(cholesky, 'col', axis=0, tiled=True)]
    ppermute x0 -> x3, waiting for transfers between devices: none -> 127 us  [the longest x2 86.4 us: body(): lower.append(lax.ppermute(lower[-1] if lower else cholesky, 'col', pairs))]
    dynamic_update_slice x1, local copies, waits for them, and re-layouts: 36.3 us -> 68.2 us  [body(): lax.dynamic_update_slice_in_dim(total, current + on_diag * piece.astype(j...]
    reshape x0 -> x1, local copies, waits for them, and re-layouts: none -> 10.6 us  [laid_out(): blocks.reshape(*dims[:dim], dims[dim] * dims[dim + 1], *dims[dim + 2:])]
  transfers between devices with their start and end apart: 4 -> 6, of which waited for: 4 -> 6; matrix products, arithmetic and copies ran while one was open for 0% -> 0% of each run, Pallas kernels for 0% -> 0%
where the time goes in v1:
time: 934 us; the launch traced here: 932 us
  waiting for transfers between devices  670 us (72%)
  matrix products  121 us (13%)
  local copies, waits for them, and re-layouts  86.5 us (9%)
  other arithmetic  35.7 us (4%)
  between operations  13.2 us (1%)
    psum x1, waiting for transfers between devices, broadcast(): return lax.psum(jnp.where(mine, x, jnp.zeros_like(x)), axis)  272 us
    reduce_scatter x1, waiting for transfers between devices, body(): lax.psum_scatter(partial_value, 'row', scatter_dimension=0, tiled=True)  185 us
    ppermute x2, waiting for transfers between devices, body(): lower.append(lax.ppermute(lower[-1] if lower else cholesky, 'col', pairs))  86.4 us
    all_gather x1, waiting for transfers between devices, body(): y_block = lax.all_gather(y_share, 'row', axis=0, tiled=True)  84.8 us
    dynamic_update_slice x1, local copies, waits for them, and re-layouts, body(): lax.dynamic_update_slice_in_dim(total, current + on_diag * piece.astype(j...  68.2 us
    dot_general x1, matrix products, body(): lax.dot_general(y_block, y_cols, (((1,), (1,)), ((), ())), preferred_elem...  63.1 us
    dot_general x1, matrix products, body(): total = jnp.dot(amplitudes, piece, preferred_element_type=jnp.float32)  57.9 us
    ppermute x1, waiting for transfers between devices, body(): upper.append(lax.ppermute(upper[-1] if upper else cholesky, 'col', back))  41 us
  transfers between devices with their start and end apart: 6, of which 6 were waited for; matrix products, arithmetic and copies ran while one was open for 0% of the time, Pallas kernels for 0%

profile of v1, /device:TPU:0, one launch (start us, length us, event | category | flops | bytes accessed | tf_op | source)
XLA Modules:
  0.0 931.6 jit_solution(11507082503690203928)
XLA Ops:
  6.5 0.0 reduce-scatter.2.cloned.1.call-start
  6.5 3.1 collective-permute-start
  9.6 2.0 collective-permute-start.2
  11.6 43.9 %collective-permute-done = bf16[768,1280]{1,0:T(8,128)(2,1)S(1)} collective-permute-done((bf16[768,1280]{1,0:T(8,128)(2,1)}, bf16[768,1280]{1,0:T(8,128)(2,1)S(1)}, u32[]{:S(2)}, u32[]{:S(2)}) %collective-permute-start) | collective-permute-done | bytes 1966112 | tf_op jit(solution)/shard_map/ppermute | solution.py:42
  55.5 0.0 collective-permute-start.1
  55.6 41.0 %collective-permute-done.2 = bf16[768,1280]{1,0:T(8,128)(2,1)} collective-permute-done((bf16[768,1280]{1,0:T(8,128)(2,1)}, bf16[768,1280]{1,0:T(8,128)(2,1)}, u32[]{:S(2)}, u32[]{:S(2)}) %collective-permute-start.2) | collective-permute-done | bytes 1966112 | tf_op jit(solution)/shard_map/ppermute | solution.py:44
  96.6 42.5 %collective-permute-done.1 = bf16[768,1280]{1,0:T(8,128)(2,1)} collective-permute-done((bf16[768,1280]{1,0:T(8,128)(2,1)S(1)}, bf16[768,1280]{1,0:T(8,128)(2,1)}, u32[]{:S(2)}, u32[]{:S(2)}) %collective-permute-start.1) | collective-permute-done | bytes 1966112 | tf_op jit(solution)/shard_map/ppermute | solution.py:42
  139.1 6.4 pad_maximum_fusion
  145.4 7.7 gather_fusion
  153.1 10.6 %copy.6 = bf16[3072,1280]{0,1:T(8,128)(2,1)} copy(bf16[3072,1280]{1,0:T(8,128)(2,1)} %bitcast.15) | data formatting | bytes 15728640 | tf_op jit(solution)/shard_map/reshape | solution.py:13
  163.7 0.0 copy-start
  163.7 57.9 %fusion.2 = f32[1280,6144]{1,0:T(8,128)} fusion(bf16[3072,1280]{1,0:T(8,128)(2,1)} %bitcast.16, bf16[6144,3072]{1,0:T(8,128)(2,1)} %param.4), kind=kOutput, calls=%fused_computation.14 | convolution fusion | flops 48318382080 | bytes 77070336 | tf_op jit(solution)/shard_map/dot_general | solution.py:50
  221.6 0.0 copy-done
  221.6 12.6 %bitcast_add_fusion = f32[3072,1280]{0,1:T(8,128)} fusion(bf16[3072,1280]{0,1:T(8,128)(2,1)S(1)} %copy-done, f32[1280,6144]{1,0:T(8,128)} %fusion.2, s32[]{:T(128)S(6)} %min.4, f32[]{:T(128)S(6)} %convert_element_type.24), kind=kLoop, calls=%fused_computation.2 | loop fusion | flops 11796480 | bytes 39321608 | tf_op jit(solution)/shard_map/add | solution.py:53
  234.2 68.2 %dynamic_update_slice.3 = f32[6144,1280]{0,1:T(8,128)} dynamic-update-slice(f32[6144,1280]{0,1:T(8,128)} %bitcast.14, f32[3072,1280]{0,1:T(8,128)} %bitcast_add_fusion, s32[]{:T(128)S(6)} %min.4, s32[]{:T(128)} %constant.57.clone.1) | dynamic-update-slice | bytes 31457284 | tf_op jit(solution)/shard_map/dynamic_update_slice | solution.py:52
  302.4 0.0 reduce-scatter.2.cloned.1.call-update
  302.4 0.0 all-gather.2.cloned.1.call-start
  302.5 185.3 %reduce-scatter.2.cloned.1.call-done = f32[768,1280]{0,1:T(8,128)} async-done(((f32[6144,1280]{0,1:T(8,128)}), f32[768,1280]{0,1:T(8,128)}) %reduce-scatter.2.cloned.1.call-update) | async-done | bytes 3932176 | tf_op jit(solution)/shard_map/reduce_scatter | solution.py:55
  487.7 3.6 convert_element_type.26
  491.3 0.0 all-gather.2.cloned.1.call-update
  491.3 0.2 all-reduce.2.cloned.1.call-start
  491.6 84.8 %all-gather.2.cloned.1.call-done = bf16[6144,1280]{0,1:T(8,128)(2,1)} async-done(((bf16[768,1280]{0,1:T(8,128)(2,1)}), bf16[6144,1280]{0,1:T(8,128)(2,1)}) %all-gather.2.cloned.1.call-update) | async-done | bytes 15728656 | tf_op jit(solution)/shard_map/all_gather | solution.py:58
  576.4 11.7 %dynamic-slice_select_fusion = bf16[3072,1280]{0,1:T(8,128)(2,1)} fusion(bf16[6144,1280]{0,1:T(8,128)(2,1)} %all-gather.2.cloned.1.call-done, s32[]{:T(128)S(6)} %select_n.60, pred[]{:T(512)S(6)} %eq.7), kind=kLoop, calls=%fused_computation.4 | loop fusion | flops 3932160 | bytes 15728645 | tf_op jit(solution)/shard_map/jit(_where)/select_n | solution.py:18
  588.1 0.0 all-reduce.2.cloned.1.call-update
  588.1 0.7 add_add_fusion.1
  588.9 0.8 add_add_fusion
  589.6 272.4 %all-reduce.2.cloned.1.call-done = bf16[3072,1280]{0,1:T(8,128)(2,1)} async-done(((bf16[3072,1280]{0,1:T(8,128)(2,1)}), bf16[3072,1280]{0,1:T(8,128)(2,1)}) %all-reduce.2.cloned.1.call-update) | async-done | bytes 7864336 | tf_op jit(solution)/shard_map/psum | solution.py:18
  862.0 63.1 %divide_convert_fusion = bf16[6144,3072]{1,0:T(8,128)(2,1)} fusion(bf16[6144,1280]{0,1:T(8,128)(2,1)} %all-gather.2.cloned.1.call-done, bf16[3072,1280]{0,1:T(8,128)(2,1)} %all-reduce.2.cloned.1.call-done, f32[3072]{0:T(1024)S(1)} %add_add_fusion.1, f32[6144]{0:T(1024)S(1)} %add_add_fusion), kind=kOutput, calls=%fused_computation.1 | convolution fusion | flops 48393879552 | bytes 61378560 | tf_op jit(solution)/shard_map/dot_general | solution.py:63
  (2 shorter events, 0.0 us)
Async XLA Ops:
  6.5 481.2 %reduce-scatter.2.cloned.1.call-start = ((), (), s32[]{:S(2)}) async-start(), calls=%async_computation.1 | async-start | bytes 35389440 | tf_op jit(solution)/shard_map/reduce_scatter | solution.py:55
  6.5 49.0 %collective-permute-start = (bf16[768,1280]{1,0:T(8,128)(2,1)}, bf16[768,1280]{1,0:T(8,128)(2,1)S(1)}, u32[]{:S(2)}, u32[]{:S(2)}) collective-permute-start(bf16[768,1280]{1,0:T(8,128)(2,1)} %param.5), channel_id=1, source_target_pairs={{0,1},{1,2},{2,3},{3,0},{4,5},{5,6},{6,7},{7,4},{8,9},{9,10},{10,1... | collective-permute-start | bytes 5898248 | tf_op jit(solution)/shard_map/ppermute | solution.py:42
  9.6 87.0 %collective-permute-start.2 = (bf16[768,1280]{1,0:T(8,128)(2,1)}, bf16[768,1280]{1,0:T(8,128)(2,1)}, u32[]{:S(2)}, u32[]{:S(2)}) collective-permute-start(bf16[768,1280]{1,0:T(8,128)(2,1)} %param.5), channel_id=1, source_target_pairs={{1,0},{2,1},{3,2},{0,3},{5,4},{6,5},{7,6},{4,7},{9,8},{10,9},{11,1... | collective-permute-start | bytes 5898248 | tf_op jit(solution)/shard_map/ppermute | solution.py:44
  55.5 83.5 %collective-permute-start.1 = (bf16[768,1280]{1,0:T(8,128)(2,1)S(1)}, bf16[768,1280]{1,0:T(8,128)(2,1)}, u32[]{:S(2)}, u32[]{:S(2)}) collective-permute-start(bf16[768,1280]{1,0:T(8,128)(2,1)S(1)} %collective-permute-done), channel_id=1, source_target_pairs={{0,1},{1,2},{2,3},{3,0},{4,5},{5,6},{6,7},{7,4},{8,9},{9,10},{10,1... | collective-permute-start | bytes 5898248 | tf_op jit(solution)/shard_map/ppermute | solution.py:42
  163.7 57.9 %copy-start = (bf16[3072,1280]{0,1:T(8,128)(2,1)S(1)}, bf16[3072,1280]{0,1:T(8,128)(2,1)}, u32[]{:S(2)}) copy-start(bf16[3072,1280]{0,1:T(8,128)(2,1)} %copy.6) | copy-start | bytes 23592964
  302.4 274.0 %all-gather.2.cloned.1.call-start = ((), (), s32[]{:S(2)}) async-start(), calls=%async_computation.2 | async-start | bytes 17694720 | tf_op jit(solution)/shard_map/all_gather | solution.py:58
  491.3 370.7 %all-reduce.2.cloned.1.call-start = ((), (), s32[]{:S(2)}) async-start(), calls=%async_computation.3 | async-start | bytes 15728640 | tf_op jit(solution)/shard_map/psum | solution.py:18
Sparse Core Ops, SparseCore 0:
  302.5 185.1 reduce-scatter.1
  491.4 84.9 all-gather.1
  588.2 273.7 all-reduce.1

commit v2 on v0

--- a/solution.py
+++ b/solution.py
@@ -9,7 +9,10 @@
 
 def broadcast(x, axis, root):
     mine = lax.axis_index(axis) == root
-    return lax.psum(jnp.where(mine, x, jnp.zeros_like(x)), axis)
+    state_sums_all = lambda local_array, bus_axis: jnp.sum(
+        jax.lax.all_gather(local_array, axis_name=bus_axis), 0
+    )
+    return state_sums_all(jnp.where(mine, x, jnp.zeros_like(x)), axis)
 
 
 def pair_gap(occ_map, vir_map):

time: 886 us -> 1150 us (1.30)
  waiting for transfers between devices: 694 us -> 947 us
  other arithmetic: 25.5 us -> 41.3 us
    all_gather x0 -> x1, waiting for transfers between devices: none -> 526 us  [broadcast(): jax.lax.all_gather(local_array, axis_name=bus_axis)]
    psum x1 -> x0, waiting for transfers between devices: 272 us -> none  [broadcast(): return lax.psum(jnp.where(mine, x, jnp.zeros_like(x)), axis)]
    reduce_sum x0 -> x1, other arithmetic: none -> 15.8 us  [broadcast(): jnp.sum(jax.lax.all_gather(local_array, axis_name=bus_axis), 0)]
where the time goes in v2:
time: 1150 us
  waiting for transfers between devices  947 us (82%)
  matrix products  115 us (10%)
  other arithmetic  41.3 us (4%)
  local copies, waits for them, and re-layouts  36.3 us (3%)
  between operations  13.2 us (1%)
    all_gather x1, waiting for transfers between devices, broadcast(): jax.lax.all_gather(local_array, axis_name=bus_axis)  526 us
    reduce_scatter x1, waiting for transfers between devices, body(): lax.psum_scatter(partial_value, 'row', scatter_dimension=0, tiled=True)  190 us
    all_gather x1, waiting for transfers between devices, body(): piece = lax.all_gather(cholesky, 'col', axis=0, tiled=True)  145 us
    all_gather x1, waiting for transfers between devices, body(): y_block = lax.all_gather(y_share, 'row', axis=0, tiled=True)  85.2 us
    dot_general x1, matrix products, body(): total = jnp.dot(amplitudes, piece, preferred_element_type=jnp.float32)  58.6 us
    dot_general x1, matrix products, body(): lax.dot_general(y_block, y_cols, (((1,), (1,)), ((), ())), preferred_elem...  56.7 us
    dynamic_update_slice x1, local copies, waits for them, and re-layouts, body(): lax.dynamic_update_slice_in_dim(total, current + on_diag * piece.astype(j...  36.3 us
  transfers between devices with their start and end apart: 4, of which 4 were waited for; matrix products, arithmetic and copies ran while one was open for 0% of the time, Pallas kernels for 0%

profile of v2, /device:TPU:0, one launch (start us, length us, event | category | flops | bytes accessed | tf_op | source)
XLA Modules:
  0.0 1153.5 jit_solution(5886756732781477928)
XLA Ops:
  6.5 0.0 all-gather.5.cloned.1.call-start
  6.5 0.7 all-gather.5.cloned.1.call-update
  7.3 0.0 reduce-scatter.2.cloned.1.call-start
  7.3 145.4 %all-gather.5.cloned.1.call-done = bf16[3072,1280]{1,0:T(8,128)(2,1)} async-done(((bf16[768,1280]{1,0:T(8,128)(2,1)}), bf16[3072,1280]{1,0:T(8,128)(2,1)}) %all-gather.5.cloned.1.call-update) | async-done | bytes 7864336 | tf_op jit(solution)/shard_map/all_gather | solution.py:33
  152.7 0.0 copy-start
  152.7 58.6 %fusion = f32[6144,1280]{1,0:T(8,128)} fusion(bf16[6144,3072]{1,0:T(8,128)(2,1)} %param.4, bf16[3072,1280]{1,0:T(8,128)(2,1)} %all-gather.5.cloned.1.call-done), kind=kOutput, calls=%fused_computation.5 | convolution fusion | flops 48318382080 | bytes 77070336 | tf_op jit(solution)/shard_map/dot_general | solution.py:35
  211.3 0.0 copy-done
  211.3 11.6 %multiply_add_fusion = f32[3072,1280]{1,0:T(8,128)} fusion(bf16[3072,1280]{1,0:T(8,128)(2,1)S(1)} %copy-done, f32[6144,1280]{1,0:T(8,128)} %fusion, s32[]{:T(128)S(6)} %min.4, f32[]{:T(128)S(6)} %convert_element_type.26), kind=kLoop, calls=%fused_computation.1 | loop fusion | flops 11796480 | bytes 39321608 | tf_op jit(solution)/shard_map/add | solution.py:38
  222.9 36.3 %dynamic_update_slice.3 = f32[6144,1280]{1,0:T(8,128)} dynamic-update-slice(f32[6144,1280]{1,0:T(8,128)} %fusion, f32[3072,1280]{1,0:T(8,128)} %multiply_add_fusion, s32[]{:T(128)S(6)} %min.4, s32[]{:T(128)} %constant.42.clone.1) | dynamic-update-slice | bytes 31457284 | tf_op jit(solution)/shard_map/dynamic_update_slice | solution.py:37
  259.3 0.0 reduce-scatter.2.cloned.1.call-update
  259.3 0.0 all-gather.7.cloned.1.call-start
  259.4 190.0 %reduce-scatter.2.cloned.1.call-done = f32[768,1280]{1,0:T(8,128)} async-done(((f32[6144,1280]{1,0:T(8,128)}), f32[768,1280]{1,0:T(8,128)}) %reduce-scatter.2.cloned.1.call-update) | async-done | bytes 3932176 | tf_op jit(solution)/shard_map/reduce_scatter | solution.py:40
  449.3 3.6 convert_element_type.28
  452.9 0.0 all-gather.7.cloned.1.call-update
  452.9 0.2 all-gather.9.cloned.1.call-start
  453.2 85.2 %all-gather.7.cloned.1.call-done = bf16[6144,1280]{1,0:T(8,128)(2,1)} async-done(((bf16[768,1280]{1,0:T(8,128)(2,1)}), bf16[6144,1280]{1,0:T(8,128)(2,1)}) %all-gather.7.cloned.1.call-update) | async-done | bytes 15728656 | tf_op jit(solution)/shard_map/all_gather | solution.py:43
  538.4 8.8 dynamic-slice_select_fusion
  547.2 0.0 all-gather.9.cloned.1.call-update
  547.2 0.7 add_add_fusion.1
  548.0 0.8 add_add_fusion
  548.7 525.7 %all-gather.9.cloned.1.call-done = bf16[12288,1280]{1,0:T(8,128)(2,1)} async-done(((bf16[3072,1280]{1,0:T(8,128)(2,1)}), bf16[12288,1280]{1,0:T(8,128)(2,1)}) %all-gather.9.cloned.1.call-update) | async-done | bytes 31457296 | tf_op jit(solution)/shard_map/all_gather | solution.py:13
  1074.5 15.8 %reduce_sum.12 = bf16[3072,1280]{1,0:T(8,128)(2,1)} reduce(bf16[4,3072,1280]{2,1,0:T(8,128)(2,1)} %bitcast.5, bf16[]{:T(256)} %constant.49.clone.1), dimensions={0}, to_apply=%region_1.2 | reduce | flops 11796480 | bytes 39321600 | tf_op jit(solution)/shard_map/reduce_sum | solution.py:12
  1090.2 56.7 %divide_convert_fusion = bf16[6144,3072]{1,0:T(8,128)(2,1)} fusion(bf16[6144,1280]{1,0:T(8,128)(2,1)} %all-gather.7.cloned.1.call-done, bf16[3072,1280]{1,0:T(8,128)(2,1)} %reduce_sum.12, f32[3072]{0:T(1024)S(1)} %add_add_fusion.1, f32[6144]{0:T(1024)S(1)} %add_add_fusion), kind=kOutput, calls=%fused_computation | convolution fusion | flops 48393879552 | bytes 61378560 | tf_op jit(solution)/shard_map/dot_general | solution.py:48
Async XLA Ops:
  6.5 146.2 %all-gather.5.cloned.1.call-start = ((), (), s32[]{:S(2)}) async-start(), calls=%async_computation.1 | async-start | bytes 9830400 | tf_op jit(solution)/shard_map/all_gather | solution.py:33
  7.3 442.1 %reduce-scatter.2.cloned.1.call-start = ((), (), s32[]{:S(2)}) async-start(), calls=%async_computation.2 | async-start | bytes 35389440 | tf_op jit(solution)/shard_map/reduce_scatter | solution.py:40
  152.7 58.6 %copy-start = (bf16[3072,1280]{1,0:T(8,128)(2,1)S(1)}, bf16[3072,1280]{1,0:T(8,128)(2,1)}, u32[]{:S(2)}) copy-start(bf16[3072,1280]{1,0:T(8,128)(2,1)} %all-gather.5.cloned.1.call-done) | copy-start | bytes 23592964
  259.3 279.1 %all-gather.7.cloned.1.call-start = ((), (), s32[]{:S(2)}) async-start(), calls=%async_computation.3 | async-start | bytes 17694720 | tf_op jit(solution)/shard_map/all_gather | solution.py:43
  452.9 621.5 %all-gather.9.cloned.1.call-start = ((), (), s32[]{:S(2)}) async-start(), calls=%async_computation.4 | async-start | bytes 39321600 | tf_op jit(solution)/shard_map/all_gather | solution.py:13
Sparse Core Ops, SparseCore 0:
  8.9 143.7 all-gather.4
  259.4 189.8 reduce-scatter.1
  453.1 85.2 all-gather.6
  547.3 527.0 all-gather.8
